TPU v7x, 32 devices: a whole 2x2x4 slice. The times are simulated.
32 devices in a mesh: fsdp: 4 (over z), ctx: 4 (over y, x), tp: 2 (over core).
Axes of the slice: x: 2, y: 2, z: 4, core: 2. Of those that a mesh axis runs over, the one named last changes fastest.
Arguments:
- tokens: bfloat16 [4096, 1024], P(('fsdp', 'ctx')), may hold values from -6 to 6
- lengths: int32 [4, 4], P('fsdp'), may hold values from 1 to 959, as said below
- norm_gain: bfloat16 [1024], P('fsdp'), may hold values from 0.5 to 1.5
- qkv_weight: bfloat16 [3, 1024, 1024], P(None, 'fsdp', 'tp'), may hold values from -0.1875 to 0.1875
- beta_weight: bfloat16 [1024, 8], P('fsdp', 'tp'), may hold values from -0.1875 to 0.1875
- conv_weight: bfloat16 [3, 4, 8, 128], P(None, None, 'tp', 'fsdp'), may hold values from -3 to 3
- head_gain: bfloat16 [128], P('fsdp'), may hold values from 0.5 to 1.5
- out_weight: bfloat16 [1024, 1024], P('tp', 'fsdp'), may hold values from -0.1875 to 0.1875
- mlp_gain: bfloat16 [1024], P('fsdp'), may hold values from 0.5 to 1.5
- gate_up_weight: bfloat16 [2, 1024, 2816], P(None, 'fsdp', 'tp'), may hold values from -0.1875 to 0.1875
- down_weight: bfloat16 [2816, 1024], P('tp', 'fsdp'), may hold values from -0.15625 to 0.15625
- cotangent: bfloat16 [4096, 1024], P(('fsdp', 'ctx')), may hold values from -6 to 6
Outputs:
- layer_out: bfloat16 [4096, 1024], P(('fsdp', 'ctx'))
- input_grad: float32 [4096, 1024], P(('fsdp', 'ctx'))
- norm_gain_grad: float32 [1024], P('fsdp')
- qkv_grad: float32 [3, 1024, 1024], P(None, 'fsdp', 'tp')
- beta_grad: float32 [1024, 8], P('fsdp', 'tp')
- conv_grad: float32 [3, 4, 8, 128], P(None, None, 'tp', 'fsdp')
- head_gain_grad: float32 [128], P('fsdp')
- out_grad: float32 [1024, 1024], P('tp', 'fsdp')
- mlp_gain_grad: float32 [1024], P('fsdp')
- gate_up_grad: float32 [2, 1024, 2816], P(None, 'fsdp', 'tp')
- down_grad: float32 [2816, 1024], P('tp', 'fsdp')
- rms: float32 [5], replicated
Inputs may be any that keep to these rules, and one draw needn't show every extreme that they name: Row g lists the 4 sequence lengths of stream g in order; they sum to at most 1024, the remaining slots at the end are padding. The second sequence of each stream ends at slot 960, so it includes a slot of the first and of the last of its 4 blocks of 256 slots.
All inputs are finite; a program needn't handle non-finite values.
Results may differ from a plain program's by a relative error of at most 0.012.
The roundings to bfloat16 on the way count: a program that leaves them out, or rounds other values in their place, can miss the bound.
Values may be sent and summed in bfloat16 or wider, within the bound.
No kernel may reach another device: no remote copies, remote signals or barrier semaphores. Data moves between devices by JAX's collectives and lax.ppermute only.
A program may use at most 128 MiB of HBM per device.

v0:
```python
import jax
import jax.numpy as jnp
from jax import lax
from jax.sharding import PartitionSpec as P

D = 1024
HD = 128
C = 64
CONV = 4
PRECISE = lax.Precision.HIGHEST
NORM_EPS = 1e-06


def passed_along(value, axis, steps):
    count = lax.axis_size(axis)
    leading, last = (max(0, -steps), min(count, count - steps))
    return lax.ppermute(value, axis, [(source, source + steps) for source in range(leading, last)])


def product(form, left, right):
    return jnp.einsum(form, left, right, precision=PRECISE)


def rounded(values):
    return lax.optimization_barrier(values.astype(jnp.bfloat16)).astype(jnp.float32)


def rms_norm(values, gain):
    return values * lax.rsqrt(jnp.mean(values * values, -1, keepdims=True) + NORM_EPS) * gain


def norm_back(values, gain, grad):
    ratio = lax.rsqrt(jnp.mean(values * values, -1, keepdims=True) + NORM_EPS)
    scaled = values * ratio
    weighted = grad * gain
    value_grad = ratio * (weighted - scaled * jnp.mean(weighted * scaled, -1, keepdims=True))
    gain_grad = jnp.sum((grad * scaled).reshape(-1, values.shape[-1]), 0)
    return (value_grad, gain_grad)


def l2_norm(values):
    return values * lax.rsqrt(jnp.sum(values * values, -1, keepdims=True) + NORM_EPS)


def seq_layout(lengths_row, first, row_count):
    ends = jnp.cumsum(lengths_row)
    places = first + jnp.arange(row_count, dtype=jnp.int32)
    passed = ends[None, :] <= places[:, None]
    begins = jnp.max(jnp.where(passed, ends[None, :], 0), -1)
    seg_ids = jnp.sum(passed.astype(jnp.int32), -1)
    valid = (places < ends[-1]).astype(jnp.float32)
    resets = places == begins
    offsets = places[:, None] - (CONV - 1) + jnp.arange(CONV, dtype=jnp.int32)[None, :]
    taps = (offsets >= begins[:, None]).astype(jnp.float32)
    return (seg_ids, resets, valid, taps)


def block_masks(seg_ids, resets):
    seg_blocks = seg_ids.reshape(-1, C)
    same_seq = (seg_blocks[:, :, None] == seg_blocks[:, None, :]).astype(jnp.float32)
    reset_count = jnp.cumsum(resets.reshape(-1, C).astype(jnp.int32), -1)
    carried = (reset_count == 0).astype(jnp.float32)
    return (same_seq, carried)


def conv_heads(extended, conv_taps, taps):
    row_count = taps.shape[0]
    total = jnp.zeros((row_count,) + extended.shape[1:], jnp.float32)
    for offset in range(CONV):
        total = (
            total
            + extended[offset : offset + row_count]
            * conv_taps[:, offset][None]
            * taps[:, offset][:, None, None]
        )
    activated = jax.nn.silu(total)
    head_count = extended.shape[2] // HD
    split_rows = activated.reshape(row_count, 3, head_count, HD)
    return (l2_norm(split_rows[:, 0]), l2_norm(split_rows[:, 1]), split_rows[:, 2])


def to_blocks(values):
    return values.reshape(values.shape[0] // C, C, values.shape[1], values.shape[2]).transpose(
        2, 0, 1, 3
    )


def beta_blocks(values):
    return values.reshape(values.shape[0] // C, C, values.shape[1]).transpose(2, 0, 1)


def from_blocks(values):
    return values.transpose(1, 2, 0, 3).reshape(-1, values.shape[0], values.shape[3])


def unit_inverse(lower):
    size_now = lower.shape[-1]
    identity = jnp.eye(size_now, dtype=jnp.float32)
    inverse = identity - lower
    power = lower
    span = 2
    while span < size_now:
        power = product("...ij,...jk->...ik", power, power)
        inverse = product("...ij,...jk->...ik", inverse, identity + power)
        span = span * 2
    return inverse


def block_terms(queries, key_rows, value_rows, beta_rows, same_seq, carried):
    wide = key_rows.shape[-1]
    last_seg = same_seq[:, -1, :]
    key_gram = product("hncd,hnmd->hncm", key_rows, key_rows)
    lower = jnp.tril(beta_rows[..., :, None] * key_gram * same_seq, -1)
    inverse = unit_inverse(lower)
    stacked = beta_rows[..., None] * jnp.concatenate([key_rows, value_rows], -1)
    solved = product("hncm,hnmd->hncd", inverse, stacked)
    w_part = solved[..., :wide]
    u_part = solved[..., wide:]
    query_key = jnp.tril(product("hncd,hnmd->hncm", queries, key_rows) * same_seq)
    keep_all = carried[:, -1]
    trans = keep_all[:, None, None] * jnp.eye(wide, dtype=jnp.float32) - product(
        "hnci,hncj->hnij", w_part * (carried * last_seg)[..., None], key_rows
    )
    push = product("hnci,hncj->hnij", u_part * last_seg[..., None], key_rows)
    return (w_part, u_part, query_key, queries, trans, push)


def run_blocks(terms, carried, start_state):
    sequenced = tuple((jnp.moveaxis(piece, 1, 0) for piece in terms)) + (carried,)

    def advance(state, pieces):
        w_now, u_now, qk_now, q_now, trans_now, push_now, carry_now = pieces
        carry_col = carry_now[None, :, None]
        from_state = product("hcd,hvd->hcv", w_now, state)
        fresh = u_now - carry_col * from_state
        output = carry_col * product("hcd,hvd->hcv", q_now, state) + product(
            "hcm,hmv->hcv", qk_now, fresh
        )
        following = product("hvk,hkj->hvj", state, trans_now) + push_now
        return (following, output)

    final_state, outputs = lax.scan(advance, start_state, sequenced)
    return (jnp.moveaxis(outputs, 0, 1), final_state)


def join_maps(earlier, later):
    return (
        product("hik,hkj->hij", earlier[0], later[0]),
        product("hvk,hkj->hvj", earlier[1], later[0]) + later[1],
    )


def row_total(values, valid):
    return jnp.sum(valid * jnp.sum(values * values, -1))


def local(
    tokens,
    lengths,
    norm_gain,
    qkv_weight,
    beta_weight,
    conv_weight,
    head_gain,
    out_weight,
    mlp_gain,
    gate_up_weight,
    down_weight,
    cotangent,
):
    row_count = tokens.shape[0]
    ctx_count = lax.axis_size("ctx")
    fsdp_count = lax.axis_size("fsdp")
    seg_ids, resets, valid, taps = seq_layout(
        lengths[0], lax.axis_index("ctx") * row_count, row_count
    )
    same_seq, carried = block_masks(seg_ids, resets)
    gathered = (
        lax.all_gather(norm_gain, "fsdp", axis=0, tiled=True),
        lax.all_gather(qkv_weight, "fsdp", axis=1, tiled=True),
        lax.all_gather(beta_weight, "fsdp", axis=0, tiled=True),
        lax.all_gather(conv_weight, "fsdp", axis=3, tiled=True),
        lax.all_gather(head_gain, "fsdp", axis=0, tiled=True),
        lax.all_gather(out_weight, "fsdp", axis=1, tiled=True),
        lax.all_gather(mlp_gain, "fsdp", axis=0, tiled=True),
        lax.all_gather(gate_up_weight, "fsdp", axis=1, tiled=True),
        lax.all_gather(down_weight, "fsdp", axis=1, tiled=True),
    )
    (
        first_gain,
        qkv_full,
        beta_full,
        conv_full,
        head_full,
        out_full,
        second_gain,
        gate_up_full,
        down_full,
    ) = gathered
    heads_local = beta_full.shape[1]
    width_local = qkv_full.shape[2]
    x_wide = tokens.astype(jnp.float32)
    first_f = first_gain.astype(jnp.float32)
    second_f = second_gain.astype(jnp.float32)
    head_f = head_full.astype(jnp.float32)
    normed_in = rms_norm(x_wide, first_f).astype(jnp.bfloat16)
    projected = jnp.einsum(
        "td,idk->tik", normed_in, qkv_full, preferred_element_type=jnp.float32
    ).astype(jnp.bfloat16)
    beta_rows = jax.nn.sigmoid(jnp.dot(normed_in, beta_full, preferred_element_type=jnp.float32))
    rim_rows = passed_along(projected[row_count - (CONV - 1) :], "ctx", 1)
    extended = jnp.concatenate([rim_rows, projected], 0).astype(jnp.float32)
    conv_local = conv_full.reshape(3, CONV, width_local).astype(jnp.float32)

    def conv_part(ext_rows, conv_taps):
        return conv_heads(ext_rows, conv_taps, taps)

    (query_raw, key_raw, value_raw), conv_pull = jax.vjp(conv_part, extended, conv_local)
    queries = rounded(query_raw)
    key_rows = rounded(key_raw)
    value_rows = rounded(value_raw)

    def prepare(query_in, key_in, value_in, beta_in):
        return block_terms(
            to_blocks(query_in) * HD ** (-0.5),
            to_blocks(key_in),
            to_blocks(value_in),
            beta_blocks(beta_in),
            same_seq,
            carried,
        )

    terms, prepare_pull = jax.vjp(prepare, queries, key_rows, value_rows, beta_rows)
    identity = jnp.broadcast_to(jnp.eye(HD, dtype=jnp.float32), (heads_local, HD, HD))
    empty_state = jnp.zeros((heads_local, HD, HD), jnp.float32)

    def compose(accum, pieces):
        return (join_maps(accum, pieces), None)

    (device_map, device_shift), ignored = lax.scan(
        compose,
        (identity, empty_state),
        (jnp.moveaxis(terms[4], 1, 0), jnp.moveaxis(terms[5], 1, 0)),
    )
    incoming = empty_state
    for repeat in range(ctx_count - 1):
        incoming = passed_along(
            product("hvk,hkj->hvj", incoming, device_map) + device_shift, "ctx", 1
        )

    def run_part(term_in, state_in):
        return run_blocks(term_in, carried, state_in)

    (out_blocks, ignored_state), run_pull = jax.vjp(run_part, terms, incoming)
    mixed_out = from_blocks(out_blocks)
    head_normed = rms_norm(mixed_out, head_f).reshape(row_count, width_local).astype(jnp.bfloat16)
    attn_rows = (
        lax.psum(jnp.dot(head_normed, out_full, preferred_element_type=jnp.float32), "tp")
        * valid[:, None]
    )
    middle = x_wide + attn_rows
    normed_mid = rms_norm(middle, second_f).astype(jnp.bfloat16)
    gate_up = jnp.einsum(
        "td,idf->tif", normed_mid, gate_up_full, preferred_element_type=jnp.float32
    )
    gate_rows = gate_up[:, 0]
    up_rows = gate_up[:, 1]
    activated = (jax.nn.silu(gate_rows) * up_rows).astype(jnp.bfloat16)
    ffn_rows = (
        lax.psum(jnp.dot(activated, down_full, preferred_element_type=jnp.float32), "tp")
        * valid[:, None]
    )
    result = middle + ffn_rows
    stat_sums = jnp.stack(
        [
            row_total(x_wide, valid),
            row_total(attn_rows, valid),
            row_total(middle, valid),
            row_total(ffn_rows, valid),
            row_total(result, valid),
            jnp.sum(valid),
        ]
    )
    out_cot = cotangent.astype(jnp.float32)
    ffn_back = (out_cot * valid[:, None]).astype(jnp.bfloat16)
    down_grad = jnp.einsum("tf,td->fd", activated, ffn_back, preferred_element_type=jnp.float32)
    act_grad = jnp.einsum("td,fd->tf", ffn_back, down_full, preferred_element_type=jnp.float32)
    gate_sig = jax.nn.sigmoid(gate_rows)
    up_grad = act_grad * gate_rows * gate_sig
    gate_grad = act_grad * up_rows * gate_sig * (1.0 + gate_rows * (1.0 - gate_sig))
    gate_up_back = jnp.stack([gate_grad, up_grad], 1).astype(jnp.bfloat16)
    gate_up_grad = jnp.einsum(
        "td,tif->idf", normed_mid, gate_up_back, preferred_element_type=jnp.float32
    )
    mid_part = jnp.einsum(
        "tif,idf->td", gate_up_back, gate_up_full, preferred_element_type=jnp.float32
    )
    mid_grad = lax.psum(mid_part, "tp")
    middle_norm_grad, second_gain_grad = norm_back(middle, second_f, mid_grad)
    middle_grad = out_cot + middle_norm_grad
    attn_back = (middle_grad * valid[:, None]).astype(jnp.bfloat16)
    out_grad = jnp.einsum("tk,td->kd", head_normed, attn_back, preferred_element_type=jnp.float32)
    head_in_grad = jnp.einsum(
        "td,kd->tk", attn_back, out_full, preferred_element_type=jnp.float32
    ).reshape(row_count, heads_local, HD)
    mixed_grad, head_gain_part = norm_back(mixed_out, head_f, head_in_grad)
    mixed_blocks = to_blocks(mixed_grad)

    def state_part(state_in):
        return run_blocks(terms, carried, state_in)[0]

    ignored_out, state_pull = jax.vjp(state_part, incoming)
    local_state = state_pull(mixed_blocks)[0]
    map_turned = jnp.swapaxes(device_map, 1, 2)
    outgoing = empty_state
    for repeat in range(ctx_count - 1):
        outgoing = passed_along(
            local_state + product("hvk,hkj->hvj", outgoing, map_turned), "ctx", -1
        )
    term_grads, ignored_grad = run_pull((mixed_blocks, outgoing))
    query_grad, key_grad, value_grad, beta_row_grad = prepare_pull(term_grads)
    logit_grad = (beta_row_grad * beta_rows * (1.0 - beta_rows)).astype(jnp.bfloat16)
    ext_grad, conv_grad_flat = conv_pull((query_grad, key_grad, value_grad))
    back_rim = passed_along(ext_grad[: CONV - 1], "ctx", -1)
    proj_grad = ext_grad[CONV - 1 :] + jnp.concatenate(
        [jnp.zeros((row_count - (CONV - 1),) + back_rim.shape[1:], jnp.float32), back_rim], 0
    )
    proj_back = proj_grad.astype(jnp.bfloat16)
    qkv_grad = jnp.einsum("td,tik->idk", normed_in, proj_back, preferred_element_type=jnp.float32)
    beta_grad = jnp.einsum("td,th->dh", normed_in, logit_grad, preferred_element_type=jnp.float32)
    in_part = jnp.einsum(
        "tik,idk->td", proj_back, qkv_full, preferred_element_type=jnp.float32
    ) + jnp.einsum("th,dh->td", logit_grad, beta_full, preferred_element_type=jnp.float32)
    in_grad, head_gain_grad = lax.psum((in_part, head_gain_part), "tp")
    x_norm_grad, first_gain_grad = norm_back(x_wide, first_f, in_grad)
    input_grad = middle_grad + x_norm_grad
    stat_rows = jnp.broadcast_to(stat_sums[None, :], (fsdp_count, stat_sums.shape[0]))
    conv_grad = conv_grad_flat.reshape(3, CONV, heads_local, HD)
    shares = (
        lax.psum_scatter(first_gain_grad, "fsdp", scatter_dimension=0, tiled=True),
        lax.psum_scatter(qkv_grad, "fsdp", scatter_dimension=1, tiled=True),
        lax.psum_scatter(beta_grad, "fsdp", scatter_dimension=0, tiled=True),
        lax.psum_scatter(conv_grad, "fsdp", scatter_dimension=3, tiled=True),
        lax.psum_scatter(head_gain_grad, "fsdp", scatter_dimension=0, tiled=True),
        lax.psum_scatter(out_grad, "fsdp", scatter_dimension=1, tiled=True),
        lax.psum_scatter(second_gain_grad, "fsdp", scatter_dimension=0, tiled=True),
        lax.psum_scatter(gate_up_grad, "fsdp", scatter_dimension=1, tiled=True),
        lax.psum_scatter(down_grad, "fsdp", scatter_dimension=1, tiled=True),
        lax.psum_scatter(stat_rows, "fsdp", scatter_dimension=0, tiled=True),
    )
    totals = lax.psum(
        (
            shares[0],
            shares[1],
            shares[2],
            shares[3],
            shares[4],
            shares[5],
            shares[6],
            shares[7],
            shares[8],
            shares[9],
        ),
        "ctx",
    )
    stat_total = totals[9][0]
    rms = jnp.sqrt(stat_total[:5] / (stat_total[5] * D))
    return (
        result.astype(jnp.bfloat16),
        input_grad,
        totals[0],
        totals[1],
        totals[2],
        totals[3],
        totals[4],
        totals[5],
        totals[6],
        totals[7],
        totals[8],
        rms,
    )


def solution(mesh):
    return jax.shard_map(
        local,
        mesh=mesh,
        in_specs=(
            P(("fsdp", "ctx"), None),
            P("fsdp", None),
            P("fsdp"),
            P(None, "fsdp", "tp"),
            P("fsdp", "tp"),
            P(None, None, "tp", "fsdp"),
            P("fsdp"),
            P("tp", "fsdp"),
            P("fsdp"),
            P(None, "fsdp", "tp"),
            P("tp", "fsdp"),
            P(("fsdp", "ctx"), None),
        ),
        out_specs=(
            P(("fsdp", "ctx"), None),
            P(("fsdp", "ctx"), None),
            P("fsdp"),
            P(None, "fsdp", "tp"),
            P("fsdp", "tp"),
            P(None, None, "tp", "fsdp"),
            P("fsdp"),
            P("tp", "fsdp"),
            P("fsdp"),
            P(None, "fsdp", "tp"),
            P("tp", "fsdp"),
            P(),
        ),
        check_vma=False,
    )
```

profile of v0, /device:TPU:0, one launch (start us, length us, event | category | flops | bytes accessed | tf_op | source)
XLA Modules:
  0.0 1154.2 jit_solution(13363397626016956386)
XLA Ops:
  10.7 12.6 %all-gather = bf16[4,1,256]{2,1,0:T(2,128)(2,1)S(1)} all-gather(bf16[1,1,256]{2,1,0:T(2,128)(2,1)S(1)} %reshape.331), channel_id=1, replica_groups=mesh['fsdp'=4,'ctx'=4,'tp'=2] {'fsdp'}, dimensions={0}, use_global_device_ids=true | all-gather | bytes 2560 | tf_op jit(solution)/shard_map/all_gather | solution.py:179
  24.0 17.8 %all_gather.30 = bf16[3,4,4,128]{2,1,0,3:T(4,128)(2,1)S(1)} all-gather(bf16[3,4,4,32]{2,1,0,3:T(4,128)(2,1)S(1)} %copy.589), channel_id=1, replica_groups=mesh['fsdp'=4,'ctx'=4,'tp'=2] {'fsdp'}, dimensions={3}, use_global_device_ids=true | all-gather | bytes 15360 | tf_op jit(solution)/shard_map/all_gather | solution.py:182
  42.4 12.2 %all_gather.28 = bf16[1024,4]{0,1:T(4,128)(2,1)S(1)} all-gather(bf16[256,4]{0,1:T(4,128)(2,1)S(1)} %copy-done.132), channel_id=1, replica_groups=mesh['fsdp'=4,'ctx'=4,'tp'=2] {'fsdp'}, dimensions={0}, use_global_device_ids=true | all-gather | bytes 10240 | tf_op jit(solution)/shard_map/all_gather | solution.py:181
  57.8 11.3 all-reduce.14
  70.2 11.6 %all-gather.7.cloned.1.call-done = bf16[3,1024,512]{2,1,0:T(8,128)(2,1)} async-done(((bf16[3,256,512]{2,1,0:T(8,128)(2,1)}), bf16[3,1024,512]{2,1,0:T(8,128)(2,1)}) %all-gather.7.cloned.1.call-update) | async-done | bytes 3145744 | tf_op jit(solution)/shard_map/all_gather | solution.py:180
  81.8 2.9 convolution_convert_fusion
  84.8 3.4 collective-permute-start
  89.8 2.9 fusion.96
  92.7 2.9 reshape.310
  95.6 2.1 fusion.237
  107.5 2.1 copy.603
  118.5 2.5 convolution_bitcast_fusion.12
  121.0 2.5 copy.609
  123.5 2.0 fusion.101
  127.2 13.8 %while.85 = (s32[]{:T(128)}, f32[4,128,128]{1,2,0:T(8,128)S(1)}, f32[4,128,128]{1,2,0:T(8,128)}, f32[4,4,128,128]{2,3,1,0:T(8,128)S(1)}, f32[4,4,128,128]{2,3,1,0:T(8,128)}, /*index=5*/s32[]{:T(128)}, s32[]{:T(128)}) while((s32[]{:T(128)}, f32[4,128,128]{1,2,0:T(8,128)S(1)}, f32[4,128,128]{1,2,0:T(8,128)}, ...), condition=%wide.region_7.8_spmd.clone, body=%wide.region_6.7_spmd.clone.sunk | while | flops 201457664 | bytes 2884699 | solution.py:240
  128.2 2.0 fusion.424
  131.6 2.0 fusion.424
  135.1 2.0 fusion.424
  138.5 2.0 fusion.424
  144.7 4.2 collective-permute-start.1
  150.2 3.1 collective-permute-done.1
  154.0 4.4 collective-permute-start.2
  159.3 2.9 collective-permute-done.2
  162.9 5.9 collective-permute-start.3
  173.9 33.4 %while.82 = (s32[]{:T(128)}, f32[4,128,128]{1,2,0:T(8,128)}, f32[4,4,64,128]{3,2,1,0:T(8,128)}, f32[4,4,128,128]{2,3,1,0:T(8,128)S(1)}, f32[4,1,64,1]{2,3,1,0:T(...) while((s32[]{:T(128)}, f32[4,128,128]{1,2,0:T(8,128)}, ...), condition=%wide.region_10.11_spmd, body=%wide.region_9.10_spmd.sunk | while | flops 226689024 | bytes 3937937 | solution.py:142
  180.1 2.1 fusion.401
  188.4 2.1 fusion.401
  196.8 2.1 fusion.401
  205.1 2.1 fusion.401
  212.4 2.7 fusion.248
  216.9 9.6 all-gather.1
  227.7 9.6 all-reduce.28.cloned.1.call-done
  239.1 107.7 %all-gather.11.cloned.1.call-done = bf16[2,1024,1408]{2,1,0:T(8,128)(2,1)} async-done(((bf16[2,256,1408]{2,1,0:T(8,128)(2,1)}), bf16[2,1024,1408]{2,1,0:T(8,128)(2,1)}) %all-gather.11.cloned.1.call-update) | async-done | bytes 5767184 | tf_op jit(solution)/shard_map/all_gather | solution.py:186
  346.8 5.9 fusion.207
  352.7 53.0 %all-gather.13.cloned.1.call-done = bf16[1408,1024]{1,0:T(8,128)(2,1)} async-done(((bf16[1408,256]{1,0:T(8,128)(2,1)}), bf16[1408,1024]{1,0:T(8,128)(2,1)}) %all-gather.13.cloned.1.call-update) | async-done | bytes 2883600 | tf_op jit(solution)/shard_map/all_gather | solution.py:187
  405.7 4.4 fusion.133
  412.2 2.7 convolution_bitcast_fusion.13
  414.9 2.8 while.83
  417.7 2.0 copy.634
  421.6 12.9 %all-reduce.34.cloned.1.call-done = (f32[256,1024]{1,0:T(8,128)}, f32[256,1024]{1,0:T(8,128)}) async-done(((f32[256,1024]{1,0:T(8,128)}, f32[256,1024]{1,0:T(8,128)}), (f32[256,1024]{1,0:T(8,128)}, f32[256,1024]{1,0:T(8,128)})) %all-reduce.34.cloned.1.call-update) | async-done | bytes 2097168 | tf_op jit(solution)/shard_map/psum | solution.py:270
  434.5 3.9 multiply_reduce_fusion.4
  441.6 2.0 fusion.226
  448.6 22.0 %while.86 = (s32[]{:T(128)}, f32[4,128,128]{1,2,0:T(8,128)}, f32[4,4,128,128]{3,2,1,0:T(8,128)}, f32[4,1,64,1]{2,3,1,0:T(1,128)S(1)}, f32[4,4,64,128]{3,2,1,0:T(...) while((s32[]{:T(128)}, f32[4,128,128]{1,2,0:T(8,128)}, ...), condition=%wide.region_21.22_spmd.clone, body=%wide.region_20.21_spmd.clone.sunk | while | flops 226787328 | bytes 2756239 | solution.py:142
  475.1 9.1 collective-permute-done.4
  486.8 9.3 collective-permute-done.5
  498.5 3.5 fusion.195
  502.1 5.2 collective-permute-done.6
  513.9 51.4 %while.84 = (s32[]{:T(128)}, f32[4,128,128]{1,2,0:T(8,128)S(1)}, f32[4,4,64,128]{3,2,0,1:T(8,128)}, f32[4,4,64,128]{3,2,0,1:T(8,128)}, f32[4,4,64,64]{2,3,1,0:T(...) while((s32[]{:T(128)}, f32[4,128,128]{1,2,0:T(8,128)S(1)}, ...), condition=%wide.region_23.24_spmd, body=%wide.region_22.23_spmd.sunk | while | flops 453312512 | bytes 9840861 | solution.py:142
  594.6 2.1 fusion.126
  606.9 4.2 collective-permute-done.7
  611.2 3.7 convolution_bitcast_fusion.10
  616.1 8.1 convolution_bitcast_fusion.9
  629.4 4.2 fusion.102
  633.7 93.4 %reduce-scatter.11.cloned.1.call-done = f32[3,256,512]{1,2,0:T(8,128)} async-done(((f32[3,1024,512]{1,2,0:T(8,128)}), f32[3,256,512]{1,2,0:T(8,128)}) %reduce-scatter.11.cloned.1.call-update) | async-done | bytes 1572880 | tf_op jit(solution)/shard_map/reduce_scatter | solution.py:341
  727.1 197.8 %reduce-scatter.15.cloned.1.call-done = f32[2,256,1408]{1,2,0:T(8,128)} async-done(((f32[2,1024,1408]{1,2,0:T(8,128)}), f32[2,256,1408]{1,2,0:T(8,128)}) %reduce-scatter.15.cloned.1.call-update) | async-done | bytes 2883600 | tf_op jit(solution)/shard_map/reduce_scatter | solution.py:347
  927.2 4.0 stack.42
  931.4 19.1 %reduce-scatter.19.cloned.1.call-done = f32[256,4]{1,0:T(8,128)} async-done(((f32[1024,4]{1,0:T(8,128)}), f32[256,4]{1,0:T(8,128)}) %reduce-scatter.19.cloned.1.call-update) | async-done | bytes 4112
  951.5 19.1 %reduce-scatter.21.cloned.1.call-done = f32[32,48]{1,0:T(8,128)} async-done(((f32[128,48]{1,0:T(8,128)}), f32[32,48]{1,0:T(8,128)}) %reduce-scatter.21.cloned.1.call-update) | async-done | bytes 6160
  971.6 19.7 %all-reduce.30.cloned.1.call-done = f32[256,1024]{1,0:T(8,128)} async-done(((f32[256,1024]{1,0:T(8,128)}), f32[256,1024]{1,0:T(8,128)}) %all-reduce.30.cloned.1.call-update) | async-done | bytes 1048592 | tf_op jit(solution)/shard_map/psum | solution.py:334
  993.1 19.0 %all-reduce.21 = (f32[1024]{0:T(1024)S(1)}, f32[128]{0:T(128)S(1)}, f32[1024]{0:T(1024)S(1)}, f32[4,6]{1,0:T(4,128)S(1)}) all-reduce(f32[1024]{0:T(1024)S(1)} %get-tuple-element.993, f32[128]{0:T(128)S(1)} %multiply_reduce_fusion.10, f32[1024]{0:T(1024)S(1)} %copy-done.116, ...), channel_id=2, replica_groups=mesh['fsdp'=4,'ctx'=4,'tp'=2] {'fsdp'}, use_global_device_ids=true, to_apply=%region_31.32.clone | all-reduce | flops 2200 | bytes 17600
  1012.3 2.4 psum.120
  1015.3 17.8 %all-reduce.19 = (f32[256]{0:T(256)}, f32[256,4]{0,1:T(4,128)}, f32[3,4,4,32]{3,2,1,0:T(4,128)}, f32[32]{0:T(128)}, f32[256]{0:T(256)}, /*index=5*/f32[1,6]{1,0:T(1,128)S(1)}) all-reduce(f32[256]{0:T(256)S(1)} %dynamic-slice.2, f32[256,4]{0,1:T(4,128)S(1)} %copy.747, ...), channel_id=1, replica_groups=mesh['fsdp'=4,'ctx'=4,'tp'=2] {'ctx'}, use_global_device_ids=true, to_apply=%region_32.33 | all-reduce | flops 3110 | bytes 24880 | tf_op jit(solution)/shard_map/psum | solution.py:351
  1036.2 103.1 %all-reduce.32.cloned.1.call-done = (f32[3,256,512]{1,2,0:T(8,128)}, f32[512,256]{1,0:T(8,128)}, f32[2,256,1408]{1,2,0:T(8,128)}, f32[1408,256]{1,0:T(8,128)}) async-done(((f32[3,256,512]{1,2,0:T(8,128)}, f32[512,256]{1,0:T(8,128)}, f32[2,256,1408]{1,2,0:T(8,128)}, f32[1408,256]{1,0:T(8,128)}), (f32[3,256,512]{1,2,0:T(8,128)}, f32[512,256]{1,0:T(8,128)}, f32[2,256,1408]{1,2,0:T(8,128)}, ...) | async-done | bytes 6422544 | tf_op jit(solution)/shard_map/psum | solution.py:351
  1139.3 3.5 copy.687
  (630 shorter events, 243.6 us)
Async XLA Ops:
  7.2 49.1 %copy-start.134 = (u32[32]{0:T(128)S(1)}, u32[32]{0:T(128)}, u32[]{:S(2)}) copy-start(u32[32]{0:T(128)} %constant.232) | copy-start | bytes 388
  7.2 16.1 %copy-start.140 = (s32[1,4]{1,0:T(1,128)S(1)}, s32[1,4]{1,0:T(1,128)}, u32[]{:S(2)}) copy-start(s32[1,4]{1,0:T(1,128)} %param.23) | copy-start | bytes 52
  7.2 16.5 %copy-start.119 = (bf16[3,4,4,32]{3,2,1,0:T(4,128)(2,1)S(1)}, bf16[3,4,4,32]{3,2,1,0:T(4,128)(2,1)}, u32[]{:S(2)}) copy-start(bf16[3,4,4,32]{3,2,1,0:T(4,128)(2,1)} %param.27) | copy-start | bytes 9220
  7.2 35.2 %copy-start.132 = (bf16[256,4]{0,1:T(4,128)(2,1)S(1)}, bf16[256,4]{0,1:T(4,128)(2,1)}, u32[]{:S(2)}) copy-start(bf16[256,4]{0,1:T(4,128)(2,1)} %param.26) | copy-start | bytes 6148
  7.2 50.3 %copy-start.141 = (bf16[32]{0:T(256)(128)(2,1)S(1)}, bf16[32]{0:T(256)(128)(2,1)}, u32[]{:S(2)}) copy-start(bf16[32]{0:T(256)(128)(2,1)} %param.28) | copy-start | bytes 196
  7.2 62.6 %copy-start.11 = (bf16[256,1024]{1,0:T(8,128)(2,1)S(1)}, bf16[256,1024]{1,0:T(8,128)(2,1)}, u32[]{:S(2)}) copy-start(bf16[256,1024]{1,0:T(8,128)(2,1)} %param.22) | copy-start | bytes 1572868
  7.3 74.5 %all-gather.7.cloned.1.call-start = ((), (), s32[]{:S(2)}) async-start(), calls=%async_computation.6 | async-start | bytes 3932160 | tf_op jit(solution)/shard_map/all_gather | solution.py:180
  8.0 204.4 %all-gather.9.cloned.1.call-start = ((), (), s32[]{:S(2)}) async-start(), calls=%async_computation.7 | async-start | bytes 1310720 | tf_op jit(solution)/shard_map/all_gather | solution.py:184
  8.7 228.6 %all-reduce.28.cloned.1.call-start = ((), (), s32[]{:S(2)}) async-start(), calls=%async_computation.8 | async-start | bytes 2097152 | tf_op jit(solution)/shard_map/psum | solution.py:258
  8.8 61.3 %copy-start.82 = (f32[128,128]{0,1:T(8,128)}, f32[128,128]{0,1:T(8,128)S(1)}, u32[]{:S(2)}) copy-start(f32[128,128]{0,1:T(8,128)S(1)} %fusion.204) | copy-start | bytes 196612
  10.7 74.1 %copy-start.106 = (f32[256]{0:T(256)}, f32[256]{0:T(256)S(1)}, u32[]{:S(2)}) copy-start(f32[256]{0:T(256)S(1)} %add_rsqrt_fusion.4) | copy-start | bytes 3076
  23.7 66.1 %copy-start.108 = (f32[256,1]{0,1:T(1,128)}, f32[256,1]{0,1:T(1,128)S(1)}, u32[]{:S(2)}) copy-start(f32[256,1]{0,1:T(1,128)S(1)} %get-tuple-element.1145) | copy-start | bytes 3076
  23.7 66.1 %copy-start.110 = (f32[256,1]{0,1:T(1,128)}, f32[256,1]{0,1:T(1,128)S(1)}, u32[]{:S(2)}) copy-start(f32[256,1]{0,1:T(1,128)S(1)} %get-tuple-element.1146) | copy-start | bytes 3076
  23.7 66.1 %copy-start.112 = (f32[256,1]{0,1:T(1,128)}, f32[256,1]{0,1:T(1,128)S(1)}, u32[]{:S(2)}) copy-start(f32[256,1]{0,1:T(1,128)S(1)} %get-tuple-element.1147) | copy-start | bytes 3076
  23.7 66.1 %copy-start.114 = (f32[256,1]{0,1:T(1,128)}, f32[256,1]{0,1:T(1,128)S(1)}, u32[]{:S(2)}) copy-start(f32[256,1]{0,1:T(1,128)S(1)} %get-tuple-element.1148) | copy-start | bytes 3076
  54.6 30.1 %copy-start.100 = (bf16[1024,4]{0,1:T(4,128)(2,1)}, bf16[1024,4]{0,1:T(4,128)(2,1)S(1)}, u32[]{:S(2)}) copy-start(bf16[1024,4]{0,1:T(4,128)(2,1)S(1)} %all_gather.28) | copy-start | bytes 24580
  56.1 13.6 %copy-start.125 = (f32[4,64]{1,0:T(4,128)}, f32[4,64]{1,0:T(4,128)S(1)}, u32[]{:S(2)}) copy-start(f32[4,64]{1,0:T(4,128)S(1)} %convert_element_type.126) | copy-start | bytes 3076
  69.7 20.1 %copy-start.84 = (f32[3,512]{1,0:T(4,128)}, f32[3,512]{1,0:T(4,128)S(1)}, u32[]{:S(2)}) copy-start(f32[3,512]{1,0:T(4,128)S(1)} %get-tuple-element.1158) | copy-start | bytes 18436
  70.2 18.1 %copy-start.117 = (f32[256,4]{0,1:T(4,128)}, f32[256,4]{0,1:T(4,128)S(1)}, u32[]{:S(2)}) copy-start(f32[256,4]{0,1:T(4,128)S(1)} %fusion.116) | copy-start | bytes 12292
  84.8 4.8 collective-permute-start
  88.3 10.2 copy-start.28
  98.5 12.1 %copy-start.5 = (f32[4,4,64,64]{2,3,1,0:T(8,128)}, f32[4,4,64,64]{2,3,1,0:T(8,128)S(1)}, u32[]{:S(2)}) copy-start(f32[4,4,64,64]{2,3,1,0:T(8,128)S(1)} %fusion.243) | copy-start | bytes 786436
  107.5 41.4 %copy-start.94 = (f32[256,4]{0,1:T(4,128)}, f32[256,4]{0,1:T(4,128)S(1)}, u32[]{:S(2)}) copy-start(f32[256,4]{0,1:T(4,128)S(1)} %fusion.147) | copy-start | bytes 12292
  141.0 13.0 %copy-start.4 = (f32[4,4,128,128]{2,3,1,0:T(8,128)}, f32[4,4,128,128]{2,3,1,0:T(8,128)S(1)}, u32[]{:S(2)}) copy-start(f32[4,4,128,128]{2,3,1,0:T(8,128)S(1)} %get-tuple-element.1647) | copy-start | bytes 3145732
  143.0 10.3 copy-start.63
  143.0 15.4 %copy-start.18 = (f32[4,4,64,256]{3,2,1,0:T(8,128)S(1)}, f32[4,4,64,256]{3,2,1,0:T(8,128)}, u32[]{:S(2)}) copy-start(f32[4,4,64,256]{3,2,1,0:T(8,128)} %copy-done.17) | copy-start | bytes 3145732
  144.7 8.6 collective-permute-start.1
  148.9 10.4 copy-start.88
  154.0 8.3 collective-permute-start.2
  162.9 9.0 collective-permute-start.3
  207.3 5.1 copy-start.2
  215.1 131.6 %all-gather.11.cloned.1.call-start = ((), (), s32[]{:S(2)}) async-start(), calls=%async_computation.9 | async-start | bytes 7208960 | tf_op jit(solution)/shard_map/all_gather | solution.py:186
  215.7 190.0 %all-gather.13.cloned.1.call-start = ((), (), s32[]{:S(2)}) async-start(), calls=%async_computation.10 | async-start | bytes 3604480 | tf_op jit(solution)/shard_map/all_gather | solution.py:187
  216.3 218.2 %all-reduce.34.cloned.1.call-start = ((), (), s32[]{:S(2)}) async-start(), calls=%async_computation.19 | async-start | bytes 4194304 | tf_op jit(solution)/shard_map/psum | solution.py:270
  239.0 113.7 %copy-start.122 = (f32[256]{0:T(256)}, f32[256]{0:T(256)S(1)}, u32[]{:S(2)}) copy-start(f32[256]{0:T(256)S(1)} %get-tuple-element.1115) | copy-start | bytes 3076
  239.0 199.4 %copy-start = (f32[256,1024]{1,0:T(8,128)}, f32[256,1024]{1,0:T(8,128)S(1)}, u32[]{:S(2)}) copy-start(f32[256,1024]{1,0:T(8,128)S(1)} %get-tuple-element.1116) | copy-start | bytes 3145732
  239.1 199.4 %copy-start.96 = (f32[256]{0:T(256)}, f32[256]{0:T(256)S(1)}, u32[]{:S(2)}) copy-start(f32[256]{0:T(256)S(1)} %add_rsqrt_fusion.3) | copy-start | bytes 3076
  405.7 6.4 copy-start.26
  414.9 218.8 %reduce-scatter.13.cloned.1.call-start = ((), (), s32[]{:S(2)}) async-start(), calls=%async_computation.13 | async-start | bytes 2621440 | tf_op jit(solution)/shard_map/reduce_scatter | solution.py:345
  447.6 186.1 %reduce-scatter.17.cloned.1.call-start = ((), (), s32[]{:S(2)}) async-start(), calls=%async_computation.15 | async-start | bytes 7208960 | tf_op jit(solution)/shard_map/reduce_scatter | solution.py:348
  472.3 23.8 %copy-start.64 = (f32[4,128,128]{2,1,0:T(8,128)S(1)}, f32[4,128,128]{2,1,0:T(8,128)}, u32[]{:S(2)}) copy-start(f32[4,128,128]{2,1,0:T(8,128)} %copy.641) | copy-start | bytes 786436
  472.3 26.2 %copy-start.73 = (bf16[256,1024]{1,0:T(8,128)(2,1)S(1)}, bf16[256,1024]{1,0:T(8,128)(2,1)}, u32[]{:S(2)}) copy-start(bf16[256,1024]{1,0:T(8,128)(2,1)} %param.33) | copy-start | bytes 1572868
  472.3 26.2 %copy-start.76 = (bf16[256,1408]{1,0:T(8,128)(2,1)S(1)}, bf16[256,1408]{1,0:T(8,128)(2,1)}, u32[]{:S(2)}) copy-start(bf16[256,1408]{1,0:T(8,128)(2,1)} %copy-done.75) | copy-start | bytes 2162692
  473.8 10.4 collective-permute-start.4
  485.5 10.6 collective-permute-start.5
  497.2 10.0 collective-permute-start.6
  502.0 225.1 %reduce-scatter.11.cloned.1.call-start = ((), (), s32[]{:S(2)}) async-start(), calls=%async_computation.12 | async-start | bytes 7864320 | tf_op jit(solution)/shard_map/reduce_scatter | solution.py:341
  513.9 51.5 %copy-start.105 = (f32[4,64]{1,0:T(4,128)S(1)}, f32[4,64]{1,0:T(4,128)}, u32[]{:S(2)}) copy-start(f32[4,64]{1,0:T(4,128)} %slice_bitcast_fusion.4) | copy-start | bytes 3076
  513.9 5.4 copy-start.3
  526.6 5.5 copy-start.3
  539.4 5.5 copy-start.3
  552.2 5.4 copy-start.3
  604.7 6.5 copy-start.12
  604.7 6.5 copy-start.107
  604.7 6.5 collective-permute-start.7
  614.9 309.9 %reduce-scatter.15.cloned.1.call-start = ((), (), s32[]{:S(2)}) async-start(), calls=%async_computation.14 | async-start | bytes 14417920 | tf_op jit(solution)/shard_map/reduce_scatter | solution.py:347
  624.3 326.3 %reduce-scatter.19.cloned.1.call-start = ((), (), s32[]{:S(2)}) async-start(), calls=%async_computation.16 | async-start | bytes 655360
  627.6 343.0 %reduce-scatter.21.cloned.1.call-start = ((), (), s32[]{:S(2)}) async-start(), calls=%async_computation.17 | async-start | bytes 81920
  629.1 362.2 %all-reduce.30.cloned.1.call-start = ((), (), s32[]{:S(2)}) async-start(), calls=%async_computation.11 | async-start | bytes 2097152 | tf_op jit(solution)/shard_map/psum | solution.py:334
  633.6 505.7 %all-reduce.32.cloned.1.call-start = ((), (), s32[]{:S(2)}) async-start(), calls=%async_computation.18 | async-start | bytes 12845056 | tf_op jit(solution)/shard_map/psum | solution.py:351
  924.9 6.2 copy-start.53
  931.2 61.9 %copy-start.116 = (f32[1024]{0:T(1024)S(1)}, f32[1024]{0:T(1024)}, u32[]{:S(2)}) copy-start(f32[1024]{0:T(1024)} %get-tuple-element.998) | copy-start | bytes 12292
  931.2 103.7 %copy-start.21 = (f32[256,1024]{1,0:T(8,128)S(1)}, f32[256,1024]{1,0:T(8,128)}, u32[]{:S(2)}) copy-start(f32[256,1024]{1,0:T(8,128)} %copy-done.20) | copy-start | bytes 3145732
  991.3 43.6 %copy-start.65 = (f32[256,1024]{1,0:T(8,128)S(1)}, f32[256,1024]{1,0:T(8,128)}, u32[]{:S(2)}) copy-start(f32[256,1024]{1,0:T(8,128)} %all-reduce.30.cloned.1.call-done) | copy-start | bytes 3145732
  (104 other events, 217.4 us)
Sparse Core Ops, SparseCore 0:
  9.7 72.0 all-gather.6
  83.3 29.4 all-gather.8
  215.2 22.0 all-reduce.27
  238.8 107.8 all-gather.10
  348.3 57.4 all-gather.12
  415.0 19.4 all-reduce.33
  447.7 45.0 reduce-scatter.12
  502.1 105.3 reduce-scatter.16
  615.1 111.9 reduce-scatter.10
  729.4 195.4 reduce-scatter.14
  927.8 22.6 reduce-scatter.18
  953.3 17.2 reduce-scatter.20
  973.5 17.7 all-reduce.29
  995.5 143.7 all-reduce.31
where the time goes:
time: 1160 us; the launch traced here: 1150 us
  waiting for transfers between devices  684 us (59%)
  matrix products  210 us (18%)
  blocking collectives  103 us (9%)
  local copies, waits for them, and re-layouts  84.7 us (7%)
  other arithmetic  28.9 us (2%)
  starting transfers between devices  24 us (2%)
  between operations  19.1 us (2%)
    reduce_scatter x1, waiting for transfers between devices, local(): lax.psum_scatter(gate_up_grad, 'fsdp', scatter_dimension=1, tiled=True)  198 us
    dot_general x123, matrix products, product(): return jnp.einsum(form, left, right, precision=PRECISE)  163 us
    all_gather x1, waiting for transfers between devices, local(): lax.all_gather(gate_up_weight, 'fsdp', axis=1, tiled=True)  108 us
    psum x1, waiting for transfers between devices, local(): lax.psum((shares[0], shares[1], shares[2], shares[3], shares[4], shares[5...  103 us
    reduce_scatter x1, waiting for transfers between devices, local(): lax.psum_scatter(qkv_grad, 'fsdp', scatter_dimension=1, tiled=True)  93.4 us
    all_gather x1, waiting for transfers between devices, local(): lax.all_gather(down_weight, 'fsdp', axis=1, tiled=True)  53 us
    unnamed x16, waiting for transfers between devices  40.8 us
    ppermute x8, waiting for transfers between devices, passed_along(): lax.ppermute(value, axis, [(source, source + steps) for source in range(l...  34.1 us
  transfers between devices with their start and end apart: 22, of which 18 were waited for; matrix products, arithmetic and copies ran while one was open for 25% of the time, Pallas kernels for 0%

commit v1 on v0

--- a/solution.py
+++ b/solution.py
@@ -9,6 +9,27 @@
 CONV = 4
 PRECISE = lax.Precision.HIGHEST
 NORM_EPS = 1e-06
+
+
+def gather_around(shard, axis, dim):
+    size, index, rows = (lax.axis_size(axis), lax.axis_index(axis), shard.shape[dim])
+    right = [(i, (i + 1) % size) for i in range(size)]
+    left = [(i, (i - 1) % size) for i in range(size)]
+    filled = jnp.zeros((*shard.shape[:dim], size * rows, *shard.shape[dim + 1 :]), shard.dtype)
+    filled = lax.dynamic_update_slice_in_dim(filled, shard, index * rows, axis=dim)
+    from_left = from_right = shard
+    middle = size // 2
+    for step in range(1, middle + 1):
+        from_left = lax.ppermute(from_left, axis, right)
+        filled = lax.dynamic_update_slice_in_dim(
+            filled, from_left, (index - step) % size * rows, axis=dim
+        )
+        if step < size - middle:
+            from_right = lax.ppermute(from_right, axis, left)
+            filled = lax.dynamic_update_slice_in_dim(
+                filled, from_right, (index + step) % size * rows, axis=dim
+            )
+    return filled
 
 
 def passed_along(value, axis, steps):
@@ -183,7 +204,7 @@
         lax.all_gather(head_gain, "fsdp", axis=0, tiled=True),
         lax.all_gather(out_weight, "fsdp", axis=1, tiled=True),
         lax.all_gather(mlp_gain, "fsdp", axis=0, tiled=True),
-        lax.all_gather(gate_up_weight, "fsdp", axis=1, tiled=True),
+        gather_around(gate_up_weight, "fsdp", 1),
         lax.all_gather(down_weight, "fsdp", axis=1, tiled=True),
     )
     (

time: 1160 us -> 1140 us (0.983)
  waiting for transfers between devices: 684 us -> 546 us
  blocking collectives: 103 us -> 174 us
  starting transfers between devices: 24 us -> 49.5 us
  local copies, waits for them, and re-layouts: 84.7 us -> 98.7 us
    all_gather x1 -> x0, waiting for transfers between devices: 108 us -> none  [local(): lax.all_gather(gate_up_weight, 'fsdp', axis=1, tiled=True)]
    all_gather x1, blocking collectives: 9.58 us -> 83.4 us  [local(): lax.all_gather(mlp_gain, 'fsdp', axis=0, tiled=True)]
    all_gather x1, waiting for transfers between devices: 53 us -> 0.01 us  [local(): lax.all_gather(down_weight, 'fsdp', axis=1, tiled=True)]
    ppermute x0 -> x3, waiting for transfers between devices: none -> 33 us  [the longest x2 33 us: gather_around(): from_left = lax.ppermute(from_left, axis, right)]
    ppermute x0 -> x3, starting transfers between devices: none -> 25.4 us  [the longest x2 21.6 us: gather_around(): from_left = lax.ppermute(from_left, axis, right)]
    unnamed x311 -> x309, local copies, waits for them, and re-layouts: 29.3 us -> 32.3 us
    unnamed x16 -> x15, waiting for transfers between devices: 40.8 us -> 40.4 us
  transfers between devices with their start and end apart: 22 -> 24, of which waited for: 18 -> 16; matrix products, arithmetic and copies ran while one was open for 25% -> 26% of each run, Pallas kernels for 0% -> 0%
where the time goes in v1:
time: 1140 us; the launch traced here: 1130 us
  waiting for transfers between devices  546 us (48%)
  matrix products  216 us (19%)
  blocking collectives  174 us (15%)
  local copies, waits for them, and re-layouts  98.7 us (9%)
  starting transfers between devices  49.5 us (4%)
  other arithmetic  28.4 us (2%)
  between operations  19 us (2%)
    reduce_scatter x1, waiting for transfers between devices, local(): lax.psum_scatter(gate_up_grad, 'fsdp', scatter_dimension=1, tiled=True)  198 us
    dot_general x123, matrix products, product(): return jnp.einsum(form, left, right, precision=PRECISE)  166 us
    psum x1, waiting for transfers between devices, local(): lax.psum((shares[0], shares[1], shares[2], shares[3], shares[4], shares[5...  103 us
    reduce_scatter x1, waiting for transfers between devices, local(): lax.psum_scatter(qkv_grad, 'fsdp', scatter_dimension=1, tiled=True)  93.2 us
    all_gather x1, blocking collectives, local(): lax.all_gather(mlp_gain, 'fsdp', axis=0, tiled=True)  83.4 us
    unnamed x15, waiting for transfers between devices  40.4 us
    ppermute x8, waiting for transfers between devices, passed_along(): lax.ppermute(value, axis, [(source, source + steps) for source in range(l...  34.2 us
    ppermute x2, waiting for transfers between devices, gather_around(): from_left = lax.ppermute(from_left, axis, right)  33 us
  transfers between devices with their start and end apart: 24, of which 16 were waited for; matrix products, arithmetic and copies ran while one was open for 26% of the time, Pallas kernels for 0%

profile of v1, /device:TPU:0, one launch (start us, length us, event | category | flops | bytes accessed | tf_op | source)
XLA Modules:
  0.0 1133.3 jit_solution(12386601565736750533)
XLA Ops:
  11.2 19.0 %all_gather.27 = bf16[3,4,4,128]{2,1,0,3:T(4,128)(2,1)S(1)} all-gather(bf16[3,4,4,32]{2,1,0,3:T(4,128)(2,1)S(1)} %copy.589), channel_id=1, replica_groups=mesh['fsdp'=4,'ctx'=4,'tp'=2] {'fsdp'}, dimensions={3}, use_global_device_ids=true | all-gather | bytes 15360 | tf_op jit(solution)/shard_map/all_gather | solution.py:203
  30.5 10.6 all-gather
  44.4 12.1 %all_gather.25 = bf16[1024,4]{0,1:T(4,128)(2,1)S(1)} all-gather(bf16[256,4]{0,1:T(4,128)(2,1)S(1)} %copy-done.132), channel_id=1, replica_groups=mesh['fsdp'=4,'ctx'=4,'tp'=2] {'fsdp'}, dimensions={0}, use_global_device_ids=true | all-gather | bytes 10240 | tf_op jit(solution)/shard_map/all_gather | solution.py:202
  58.1 10.0 all-reduce.14
  69.2 8.9 all-gather.6.cloned.1.call-done
  78.1 2.9 convolution_convert_fusion
  81.1 3.4 collective-permute-start
  86.2 2.9 fusion.96
  89.1 2.9 reshape.310
  114.8 2.4 fusion.101
  118.9 3.1 convolution_bitcast_fusion.12
  122.0 2.5 copy.609
  124.5 13.7 %while.85 = (s32[]{:T(128)}, f32[4,128,128]{1,2,0:T(8,128)S(1)}, f32[4,128,128]{1,2,0:T(8,128)}, f32[4,4,128,128]{2,3,1,0:T(8,128)S(1)}, f32[4,4,128,128]{2,3,1,0:T(8,128)}, /*index=5*/s32[]{:T(128)}, s32[]{:T(128)}) while((s32[]{:T(128)}, f32[4,128,128]{1,2,0:T(8,128)S(1)}, f32[4,128,128]{1,2,0:T(8,128)}, ...), condition=%wide.region_7.8_spmd.clone, body=%wide.region_6.7_spmd.clone.sunk | while | flops 201457664 | bytes 2885218 | solution.py:261
  140.2 4.2 collective-permute-start.1
  145.9 3.1 collective-permute-done.1
  149.7 4.4 collective-permute-start.2
  155.0 2.9 collective-permute-done.2
  158.6 6.0 collective-permute-start.3
  169.7 33.4 %while.82 = (s32[]{:T(128)}, f32[4,128,128]{1,2,0:T(8,128)}, f32[4,4,64,128]{3,2,1,0:T(8,128)}, f32[4,4,128,128]{2,3,1,0:T(8,128)S(1)}, f32[4,1,64,1]{2,3,1,0:T(...) while((s32[]{:T(128)}, f32[4,128,128]{1,2,0:T(8,128)}, ...), condition=%wide.region_10.11_spmd, body=%wide.region_9.10_spmd.sunk | while | flops 226689024 | bytes 3937437 | solution.py:163
  208.3 2.7 fusion.248
  211.7 3.8 collective-permute-start.5
  215.5 33.0 %collective-permute-done.4 = bf16[2,256,1408]{2,1,0:T(8,128)(2,1)} collective-permute-done((bf16[2,256,1408]{2,1,0:T(8,128)(2,1)}, bf16[2,256,1408]{2,1,0:T(8,128)(2,1)}, u32[]{:S(2)}, u32[]{:S(2)}) %collective-permute-start.4) | collective-permute-done | bytes 1441824 | tf_op jit(solution)/shard_map/ppermute | solution.py:23
  248.6 21.5 %collective-permute-start.6 = (bf16[2,256,1408]{2,1,0:T(8,128)(2,1)}, bf16[2,256,1408]{2,1,0:T(8,128)(2,1)}, u32[]{:S(2)}, u32[]{:S(2)}) collective-permute-start(bf16[2,256,1408]{2,1,0:T(8,128)(2,1)} %collective-permute-done.4), channel_id=1, source_target_pairs={{0,8},{8,16},{16,24},{24,0},{1,9},{9,17},{17,25},{25,1},{2,10},{10... | collective-permute-start | bytes 4325384 | tf_op jit(solution)/shard_map/ppermute | solution.py:23
  270.7 83.4 %all-gather.1 = bf16[4,1,256]{2,1,0:T(2,128)(2,1)S(1)} all-gather(bf16[1,1,256]{2,1,0:T(2,128)(2,1)S(1)} %reshape.333), channel_id=1, replica_groups=mesh['fsdp'=4,'ctx'=4,'tp'=2] {'fsdp'}, dimensions={0}, use_global_device_ids=true | all-gather | bytes 2560 | tf_op jit(solution)/shard_map/all_gather | solution.py:206
  355.4 2.9 broadcast_in_dim.188
  359.4 2.6 constant_dynamic-update-slice_fusion.4
  362.0 2.6 constant_dynamic-update-slice_fusion.3
  364.6 2.6 constant_dynamic-update-slice_fusion.2
  369.0 6.3 fusion.207
  375.3 4.3 fusion.133
  379.6 6.1 convolution_bitcast_fusion.13
  387.8 2.8 while.83
  390.6 2.5 copy.631
  394.8 15.7 %all-reduce.34.cloned.1.call-done = (f32[256,1024]{1,0:T(8,128)}, f32[256,1024]{1,0:T(8,128)}) async-done(((f32[256,1024]{1,0:T(8,128)}, f32[256,1024]{1,0:T(8,128)}), (f32[256,1024]{1,0:T(8,128)}, f32[256,1024]{1,0:T(8,128)})) %all-reduce.34.cloned.1.call-update) | async-done | bytes 2097168 | tf_op jit(solution)/shard_map/psum | solution.py:291
  410.4 3.9 multiply_reduce_fusion.4
  424.5 22.0 %while.86 = (s32[]{:T(128)}, f32[4,128,128]{1,2,0:T(8,128)}, f32[4,4,128,128]{3,2,1,0:T(8,128)}, f32[4,1,64,1]{2,3,1,0:T(1,128)S(1)}, f32[4,4,64,128]{3,2,1,0:T(...) while((s32[]{:T(128)}, f32[4,128,128]{1,2,0:T(8,128)}, ...), condition=%wide.region_21.22_spmd.clone, body=%wide.region_20.21_spmd.clone.sunk | while | flops 226787328 | bytes 2756247 | solution.py:163
  433.3 2.2 convolution_add_fusion.28
  438.8 2.2 convolution_add_fusion.28
  451.1 9.1 collective-permute-done.7
  462.8 9.3 collective-permute-done.8
  474.6 3.5 fusion.195
  478.1 5.2 collective-permute-done.9
  490.0 55.3 %while.84 = (s32[]{:T(128)}, f32[4,128,128]{1,2,0:T(8,128)S(1)}, f32[4,4,64,128]{3,2,0,1:T(8,128)}, f32[4,4,64,128]{3,2,0,1:T(8,128)}, f32[4,4,64,64]{2,3,1,0:T(...) while((s32[]{:T(128)}, f32[4,128,128]{1,2,0:T(8,128)S(1)}, ...), condition=%wide.region_23.24_spmd, body=%wide.region_22.23_spmd.sunk | while | flops 453312512 | bytes 9840613 | solution.py:163
  490.7 2.3 fusion.419
  504.5 2.3 fusion.419
  518.1 2.3 fusion.419
  531.9 2.3 fusion.419
  545.3 2.5 convolution_multiply_fusion.2
  585.4 4.3 collective-permute-done.10
  589.7 3.9 convolution_bitcast_fusion.10
  594.8 8.1 convolution_bitcast_fusion.9
  608.2 4.2 fusion.102
  612.5 93.2 %reduce-scatter.11.cloned.1.call-done = f32[3,256,512]{1,2,0:T(8,128)} async-done(((f32[3,1024,512]{1,2,0:T(8,128)}), f32[3,256,512]{1,2,0:T(8,128)}) %reduce-scatter.11.cloned.1.call-update) | async-done | bytes 1572880 | tf_op jit(solution)/shard_map/reduce_scatter | solution.py:362
  705.7 198.0 %reduce-scatter.15.cloned.1.call-done = f32[2,256,1408]{1,2,0:T(8,128)} async-done(((f32[2,1024,1408]{1,2,0:T(8,128)}), f32[2,256,1408]{1,2,0:T(8,128)}) %reduce-scatter.15.cloned.1.call-update) | async-done | bytes 2883600 | tf_op jit(solution)/shard_map/reduce_scatter | solution.py:368
  905.9 4.0 stack.42
  910.1 19.1 %reduce-scatter.19.cloned.1.call-done = f32[256,4]{1,0:T(8,128)} async-done(((f32[1024,4]{1,0:T(8,128)}), f32[256,4]{1,0:T(8,128)}) %reduce-scatter.19.cloned.1.call-update) | async-done | bytes 4112
  930.2 19.2 %reduce-scatter.21.cloned.1.call-done = f32[32,48]{1,0:T(8,128)} async-done(((f32[128,48]{1,0:T(8,128)}), f32[32,48]{1,0:T(8,128)}) %reduce-scatter.21.cloned.1.call-update) | async-done | bytes 6160
  950.3 19.6 %all-reduce.30.cloned.1.call-done = f32[256,1024]{1,0:T(8,128)} async-done(((f32[256,1024]{1,0:T(8,128)}), f32[256,1024]{1,0:T(8,128)}) %all-reduce.30.cloned.1.call-update) | async-done | bytes 1048592 | tf_op jit(solution)/shard_map/psum | solution.py:355
  971.7 19.0 %all-reduce.21 = (f32[1024]{0:T(1024)S(1)}, f32[128]{0:T(128)S(1)}, f32[1024]{0:T(1024)S(1)}, f32[4,6]{1,0:T(4,128)S(1)}) all-reduce(f32[1024]{0:T(1024)S(1)} %get-tuple-element.993, f32[128]{0:T(128)S(1)} %multiply_reduce_fusion.10, f32[1024]{0:T(1024)S(1)} %copy-done.117, ...), channel_id=2, replica_groups=mesh['fsdp'=4,'ctx'=4,'tp'=2] {'fsdp'}, use_global_device_ids=true, to_apply=%region_31.32.clone | all-reduce | flops 2200 | bytes 17600
  990.8 2.4 psum.120
  993.8 17.8 %all-reduce.19 = (f32[256]{0:T(256)}, f32[256,4]{0,1:T(4,128)}, f32[3,4,4,32]{3,2,1,0:T(4,128)}, f32[32]{0:T(128)}, f32[256]{0:T(256)}, /*index=5*/f32[1,6]{1,0:T(1,128)S(1)}) all-reduce(f32[256]{0:T(256)S(1)} %dynamic-slice.2, f32[256,4]{0,1:T(4,128)S(1)} %copy.747, ...), channel_id=1, replica_groups=mesh['fsdp'=4,'ctx'=4,'tp'=2] {'ctx'}, use_global_device_ids=true, to_apply=%region_32.33 | all-reduce | flops 3110 | bytes 24880 | tf_op jit(solution)/shard_map/psum | solution.py:372
  1014.7 103.3 %all-reduce.32.cloned.1.call-done = (f32[3,256,512]{1,2,0:T(8,128)}, f32[512,256]{1,0:T(8,128)}, f32[2,256,1408]{1,2,0:T(8,128)}, f32[1408,256]{1,0:T(8,128)}) async-done(((f32[3,256,512]{1,2,0:T(8,128)}, f32[512,256]{1,0:T(8,128)}, f32[2,256,1408]{1,2,0:T(8,128)}, f32[1408,256]{1,0:T(8,128)}), (f32[3,256,512]{1,2,0:T(8,128)}, f32[512,256]{1,0:T(8,128)}, f32[2,256,1408]{1,2,0:T(8,128)}, ...) | async-done | bytes 6422544 | tf_op jit(solution)/shard_map/psum | solution.py:372
  1118.0 3.0 copy.686
  1121.1 3.5 copy.687
  (636 shorter events, 252.3 us)
Async XLA Ops:
  7.2 49.4 %copy-start.134 = (u32[32]{0:T(128)S(1)}, u32[32]{0:T(128)}, u32[]{:S(2)}) copy-start(u32[32]{0:T(128)} %constant.265) | copy-start | bytes 388
  7.2 23.3 %copy-start.139 = (bf16[256]{0:T(256)(128)(2,1)S(1)}, bf16[256]{0:T(256)(128)(2,1)}, u32[]{:S(2)}) copy-start(bf16[256]{0:T(256)(128)(2,1)} %param.24) | copy-start | bytes 1540
  7.2 34.0 %copy-start.11 = (bf16[256,1024]{1,0:T(8,128)(2,1)S(1)}, bf16[256,1024]{1,0:T(8,128)(2,1)}, u32[]{:S(2)}) copy-start(bf16[256,1024]{1,0:T(8,128)(2,1)} %param.22) | copy-start | bytes 1572868
  7.2 37.2 %copy-start.132 = (bf16[256,4]{0,1:T(4,128)(2,1)S(1)}, bf16[256,4]{0,1:T(4,128)(2,1)}, u32[]{:S(2)}) copy-start(bf16[256,4]{0,1:T(4,128)(2,1)} %param.26) | copy-start | bytes 6148
  7.2 50.6 %copy-start.140 = (bf16[32]{0:T(256)(128)(2,1)S(1)}, bf16[32]{0:T(256)(128)(2,1)}, u32[]{:S(2)}) copy-start(bf16[32]{0:T(256)(128)(2,1)} %param.28) | copy-start | bytes 196
  7.2 70.9 %all-gather.6.cloned.1.call-start = ((), (), s32[]{:S(2)}) async-start(), calls=%async_computation.6 | async-start | bytes 3932160 | tf_op jit(solution)/shard_map/all_gather | solution.py:201
  8.0 200.3 %all-gather.8.cloned.1.call-start = ((), (), s32[]{:S(2)}) async-start(), calls=%async_computation.7 | async-start | bytes 1310720 | tf_op jit(solution)/shard_map/all_gather | solution.py:205
  8.7 358.5 %all-reduce.28.cloned.1.call-start = ((), (), s32[]{:S(2)}) async-start(), calls=%async_computation.8 | async-start | bytes 2097152 | tf_op jit(solution)/shard_map/psum | solution.py:279
  8.8 60.4 %copy-start.82 = (f32[128,128]{0,1:T(8,128)}, f32[128,128]{0,1:T(8,128)S(1)}, u32[]{:S(2)}) copy-start(f32[128,128]{0,1:T(8,128)S(1)} %fusion.204) | copy-start | bytes 196612
  10.3 75.9 %copy-start.109 = (f32[256,1]{0,1:T(1,128)}, f32[256,1]{0,1:T(1,128)S(1)}, u32[]{:S(2)}) copy-start(f32[256,1]{0,1:T(1,128)S(1)} %get-tuple-element.1145) | copy-start | bytes 3076
  10.3 75.9 %copy-start.111 = (f32[256,1]{0,1:T(1,128)}, f32[256,1]{0,1:T(1,128)S(1)}, u32[]{:S(2)}) copy-start(f32[256,1]{0,1:T(1,128)S(1)} %get-tuple-element.1146) | copy-start | bytes 3076
  10.3 75.9 %copy-start.113 = (f32[256,1]{0,1:T(1,128)}, f32[256,1]{0,1:T(1,128)S(1)}, u32[]{:S(2)}) copy-start(f32[256,1]{0,1:T(1,128)S(1)} %get-tuple-element.1147) | copy-start | bytes 3076
  10.3 75.9 %copy-start.115 = (f32[256,1]{0,1:T(1,128)}, f32[256,1]{0,1:T(1,128)S(1)}, u32[]{:S(2)}) copy-start(f32[256,1]{0,1:T(1,128)S(1)} %get-tuple-element.1148) | copy-start | bytes 3076
  41.9 39.1 %copy-start.107 = (f32[256]{0:T(256)}, f32[256]{0:T(256)S(1)}, u32[]{:S(2)}) copy-start(f32[256]{0:T(256)S(1)} %add_rsqrt_fusion.4) | copy-start | bytes 3076
  56.5 24.5 %copy-start.101 = (bf16[1024,4]{0,1:T(4,128)(2,1)}, bf16[1024,4]{0,1:T(4,128)(2,1)S(1)}, u32[]{:S(2)}) copy-start(bf16[1024,4]{0,1:T(4,128)(2,1)S(1)} %all_gather.25) | copy-start | bytes 24580
  68.1 13.0 %copy-start.127 = (f32[128]{0:T(128)}, f32[128]{0:T(128)S(1)}, u32[]{:S(2)}) copy-start(f32[128]{0:T(128)S(1)} %convert_element_type.141) | copy-start | bytes 1540
  68.7 17.4 %copy-start.85 = (f32[3,512]{1,0:T(4,128)}, f32[3,512]{1,0:T(4,128)S(1)}, u32[]{:S(2)}) copy-start(f32[3,512]{1,0:T(4,128)S(1)} %get-tuple-element.1158) | copy-start | bytes 18436
  69.2 16.3 %copy-start.118 = (f32[256,4]{0,1:T(4,128)}, f32[256,4]{0,1:T(4,128)S(1)}, u32[]{:S(2)}) copy-start(f32[256,4]{0,1:T(4,128)S(1)} %fusion.116) | copy-start | bytes 12292
  81.1 4.8 collective-permute-start
  84.6 10.2 copy-start.27
  94.8 11.8 %copy-start.5 = (f32[4,4,64,64]{2,3,1,0:T(8,128)}, f32[4,4,64,64]{2,3,1,0:T(8,128)S(1)}, u32[]{:S(2)}) copy-start(f32[4,4,64,64]{2,3,1,0:T(8,128)S(1)} %fusion.243) | copy-start | bytes 786436
  138.2 11.4 %copy-start.4 = (f32[4,4,128,128]{2,3,1,0:T(8,128)}, f32[4,4,128,128]{2,3,1,0:T(8,128)S(1)}, u32[]{:S(2)}) copy-start(f32[4,4,128,128]{2,3,1,0:T(8,128)S(1)} %get-tuple-element.1646) | copy-start | bytes 3145732
  139.5 6.2 copy-start.24
  139.5 14.6 %copy-start.18 = (f32[4,4,64,256]{3,2,1,0:T(8,128)S(1)}, f32[4,4,64,256]{3,2,1,0:T(8,128)}, u32[]{:S(2)}) copy-start(f32[4,4,64,256]{3,2,1,0:T(8,128)} %copy-done.17) | copy-start | bytes 3145732
  140.2 8.8 collective-permute-start.1
  145.7 9.4 copy-start.95
  145.7 9.3 copy-start.89
  149.7 8.3 collective-permute-start.2
  158.6 7.8 copy-start.29
  158.6 9.2 collective-permute-start.3
  208.3 61.9 %copy-start.137 = (s32[4,1]{0,1:T(1,128)S(1)}, s32[4,1]{0,1:T(1,128)}, u32[]{:S(2)}) copy-start(s32[4,1]{0,1:T(1,128)} %copy-done.136) | copy-start | bytes 52
  208.3 62.4 %copy-start.141 = (bf16[256]{0:T(256)(128)(2,1)S(1)}, bf16[256]{0:T(256)(128)(2,1)}, u32[]{:S(2)}) copy-start(bf16[256]{0:T(256)(128)(2,1)} %param.30) | copy-start | bytes 1540
  211.0 164.2 %all-gather.10.cloned.1.call-start = ((), (), s32[]{:S(2)}) async-start(), calls=%async_computation.9 | async-start | bytes 3604480 | tf_op jit(solution)/shard_map/all_gather | solution.py:208
  211.6 198.8 %all-reduce.34.cloned.1.call-start = ((), (), s32[]{:S(2)}) async-start(), calls=%async_computation.18 | async-start | bytes 4194304 | tf_op jit(solution)/shard_map/psum | solution.py:291
  211.7 36.9 %collective-permute-start.4 = (bf16[2,256,1408]{2,1,0:T(8,128)(2,1)}, bf16[2,256,1408]{2,1,0:T(8,128)(2,1)}, u32[]{:S(2)}, u32[]{:S(2)}) collective-permute-start(bf16[2,256,1408]{2,1,0:T(8,128)(2,1)} %param.31), channel_id=1, source_target_pairs={{0,8},{8,16},{16,24},{24,0},{1,9},{9,17},{17,25},{25,1},{2,10},{10... | collective-permute-start | bytes 4325384 | tf_op jit(solution)/shard_map/ppermute | solution.py:23
  211.7 150.3 %collective-permute-start.5 = (bf16[2,256,1408]{2,1,0:T(8,128)(2,1)}, bf16[2,256,1408]{2,1,0:T(8,128)(2,1)}, u32[]{:S(2)}, u32[]{:S(2)}) collective-permute-start(bf16[2,256,1408]{2,1,0:T(8,128)(2,1)} %param.31), channel_id=1, source_target_pairs={{0,24},{8,0},{16,8},{24,16},{1,25},{9,1},{17,9},{25,17},{2,26},{10... | collective-permute-start | bytes 4325384 | tf_op jit(solution)/shard_map/ppermute | solution.py:28
  248.6 116.0 %collective-permute-start.6 = (bf16[2,256,1408]{2,1,0:T(8,128)(2,1)}, bf16[2,256,1408]{2,1,0:T(8,128)(2,1)}, u32[]{:S(2)}, u32[]{:S(2)}) collective-permute-start(bf16[2,256,1408]{2,1,0:T(8,128)(2,1)} %collective-permute-done.4), channel_id=1, source_target_pairs={{0,8},{8,16},{16,24},{24,0},{1,9},{9,17},{17,25},{25,1},{2,10},{10... | collective-permute-start | bytes 4325384 | tf_op jit(solution)/shard_map/ppermute | solution.py:23
  368.9 6.3 copy-start.122
  368.9 45.4 %copy-start = (f32[256,1024]{1,0:T(8,128)}, f32[256,1024]{1,0:T(8,128)S(1)}, u32[]{:S(2)}) copy-start(f32[256,1024]{1,0:T(8,128)S(1)} %get-tuple-element.1116) | copy-start | bytes 3145732
  369.0 45.4 %copy-start.97 = (f32[256]{0:T(256)}, f32[256]{0:T(256)S(1)}, u32[]{:S(2)}) copy-start(f32[256]{0:T(256)S(1)} %add_rsqrt_fusion.3) | copy-start | bytes 3076
  379.6 6.2 copy-start.80
  379.6 6.2 copy-start.81
  379.6 6.1 copy-start.74
  387.7 224.7 %reduce-scatter.13.cloned.1.call-start = ((), (), s32[]{:S(2)}) async-start(), calls=%async_computation.12 | async-start | bytes 2621440 | tf_op jit(solution)/shard_map/reduce_scatter | solution.py:366
  423.6 188.9 %reduce-scatter.17.cloned.1.call-start = ((), (), s32[]{:S(2)}) async-start(), calls=%async_computation.14 | async-start | bytes 7208960 | tf_op jit(solution)/shard_map/reduce_scatter | solution.py:369
  448.3 23.8 %copy-start.64 = (f32[4,128,128]{2,1,0:T(8,128)S(1)}, f32[4,128,128]{2,1,0:T(8,128)}, u32[]{:S(2)}) copy-start(f32[4,128,128]{2,1,0:T(8,128)} %copy.641) | copy-start | bytes 786436
  448.3 26.2 %copy-start.73 = (bf16[256,1024]{1,0:T(8,128)(2,1)S(1)}, bf16[256,1024]{1,0:T(8,128)(2,1)}, u32[]{:S(2)}) copy-start(bf16[256,1024]{1,0:T(8,128)(2,1)} %param.33) | copy-start | bytes 1572868
  448.3 26.2 %copy-start.75 = (bf16[256,1408]{1,0:T(8,128)(2,1)S(1)}, bf16[256,1408]{1,0:T(8,128)(2,1)}, u32[]{:S(2)}) copy-start(bf16[256,1408]{1,0:T(8,128)(2,1)} %copy-done.74) | copy-start | bytes 2162692
  449.8 10.4 collective-permute-start.7
  461.5 10.6 collective-permute-start.8
  473.2 10.0 collective-permute-start.9
  478.0 227.6 %reduce-scatter.11.cloned.1.call-start = ((), (), s32[]{:S(2)}) async-start(), calls=%async_computation.11 | async-start | bytes 7864320 | tf_op jit(solution)/shard_map/reduce_scatter | solution.py:362
  490.0 55.3 %copy-start.104 = (f32[4,64]{1,0:T(4,128)S(1)}, f32[4,64]{1,0:T(4,128)}, u32[]{:S(2)}) copy-start(f32[4,64]{1,0:T(4,128)} %get-tuple-element.1119) | copy-start | bytes 3076
  583.2 6.6 copy-start.12
  583.2 6.5 copy-start.108
  583.2 6.5 collective-permute-start.10
  593.6 310.0 %reduce-scatter.15.cloned.1.call-start = ((), (), s32[]{:S(2)}) async-start(), calls=%async_computation.13 | async-start | bytes 14417920 | tf_op jit(solution)/shard_map/reduce_scatter | solution.py:368
  603.0 326.2 %reduce-scatter.19.cloned.1.call-start = ((), (), s32[]{:S(2)}) async-start(), calls=%async_computation.15 | async-start | bytes 655360
  606.4 342.9 %reduce-scatter.21.cloned.1.call-start = ((), (), s32[]{:S(2)}) async-start(), calls=%async_computation.16 | async-start | bytes 81920
  607.9 362.0 %all-reduce.30.cloned.1.call-start = ((), (), s32[]{:S(2)}) async-start(), calls=%async_computation.10 | async-start | bytes 2097152 | tf_op jit(solution)/shard_map/psum | solution.py:355
  612.4 505.7 %all-reduce.32.cloned.1.call-start = ((), (), s32[]{:S(2)}) async-start(), calls=%async_computation.17 | async-start | bytes 12845056 | tf_op jit(solution)/shard_map/psum | solution.py:372
  909.8 61.8 %copy-start.117 = (f32[1024]{0:T(1024)S(1)}, f32[1024]{0:T(1024)}, u32[]{:S(2)}) copy-start(f32[1024]{0:T(1024)} %get-tuple-element.998) | copy-start | bytes 12292
  909.8 103.6 %copy-start.21 = (f32[256,1024]{1,0:T(8,128)S(1)}, f32[256,1024]{1,0:T(8,128)}, u32[]{:S(2)}) copy-start(f32[256,1024]{1,0:T(8,128)} %copy-done.20) | copy-start | bytes 3145732
  969.9 43.6 %copy-start.65 = (f32[256,1024]{1,0:T(8,128)S(1)}, f32[256,1024]{1,0:T(8,128)}, u32[]{:S(2)}) copy-start(f32[256,1024]{1,0:T(8,128)} %all-reduce.30.cloned.1.call-done) | copy-start | bytes 3145732
  (105 other events, 235.7 us)
Sparse Core Ops, SparseCore 0:
  9.6 68.4 all-gather.5
  79.7 29.1 all-gather.7
  211.2 21.5 all-reduce.27
  234.2 116.0 all-gather.9
  387.8 22.5 all-reduce.33
  423.7 45.0 reduce-scatter.12
  478.2 105.3 reduce-scatter.16
  593.7 111.8 reduce-scatter.10
  708.1 195.4 reduce-scatter.14
  906.4 22.6 reduce-scatter.18
  932.1 17.1 reduce-scatter.20
  952.1 17.7 all-reduce.29
  974.2 143.7 all-reduce.31
